TPU v7x, 32 devices: a whole 2x2x4 slice. The times are simulated.
32 devices in a mesh: batch: 8 (over z, y), head: 4 (over x, core).
Axes of the slice: x: 2, y: 2, z: 4, core: 2. Of those that a mesh axis runs over, the one named last changes fastest.
Arguments:
- tokens: bfloat16 [16384, 768], P(('batch', 'head')), may hold values from -6 to 6
- cotangent: bfloat16 [16384, 768], P(('batch', 'head')), may hold values from -6 to 6
- lengths: int32 [32], P('batch'), may hold values from 16 to 512, as said below
- labels: int32 [32], P('batch'), may hold values from 0 to 2
- w_qkv: bfloat16 [768, 2304], replicated, may hold values from -0.21875 to 0.21875
- w_out: bfloat16 [768, 768], replicated, may hold values from -0.875 to 0.875
- w_up: bfloat16 [768, 3072], replicated, may hold values from -0.21875 to 0.21875
- w_down: bfloat16 [3072, 768], replicated, may hold values from -0.109375 to 0.109375
- w_pool: bfloat16 [768, 768], replicated, may hold values from -0.21875 to 0.21875
- w_class: bfloat16 [3, 768], replicated, may hold values from -0.625 to 0.625
- biases: float32 [7, 768], replicated, may hold values from -3 to 3
- norm_gains: float32 [2, 768], replicated, may hold values from 0.25 to 1.75
- bias_up: float32 [3072], replicated, may hold values from -3 to 3
Outputs:
- out: bfloat16 [16384, 768], P(('batch', 'head'))
- grad_tokens: bfloat16 [16384, 768], P(('batch', 'head'))
- losses: float32 [32], P(('batch', 'head'))
- g_qkv: float32 [768, 2304], P(None, ('batch', 'head'))
- g_out: float32 [768, 768], P(None, ('batch', 'head'))
- g_up: float32 [768, 3072], P(None, ('batch', 'head'))
- g_down: float32 [3072, 768], P(None, ('batch', 'head'))
- g_pool: float32 [768, 768], P(None, ('batch', 'head'))
- g_class: float32 [3, 768], P(None, ('batch', 'head'))
- g_biases: float32 [6, 768], P(None, ('batch', 'head'))
- g_gains: float32 [2, 768], P(None, ('batch', 'head'))
- g_bias_up: float32 [3072], P(('batch', 'head'))
- g_pool_bias: float32 [768], P(('batch', 'head'))
Inputs may be any that keep to these rules, and one draw needn't show every extreme that they name: `lengths`: some sequence has exactly 512 and some exactly 16 positions.
All inputs are finite; a program needn't handle non-finite values.
Results may differ from a plain program's by a relative error of at most 0.014.
Values may be sent and summed in bfloat16 or wider, within the bound.
A program may use at most 192 MiB of HBM per device.

v0:
```python
import jax
import jax.numpy as jnp
from jax import lax
from jax.sharding import PartitionSpec as P

D = 768
HEADS = 12
HEAD_DIM = 64
CLASSES = 3
SLOT = 512


def layer_norm(hidden, gain, shift):
    center = hidden - jnp.mean(hidden, axis=-1, keepdims=True)
    spread = jnp.mean(center * center, axis=-1, keepdims=True)
    return center * lax.rsqrt(spread + 1e-12) * gain + shift


def exact_gelu(hidden):
    return jax.nn.gelu(hidden, approximate=False)


def inner(left, right):
    return lax.dot_general(
        left, right, (((0,), (0,)), ((), ())), preferred_element_type=jnp.float32
    )


def against(left, right):
    return lax.dot_general(
        left, right, (((1,), (1,)), ((), ())), preferred_element_type=jnp.float32
    )


def exact(left, right):
    return jnp.dot(left, right, precision=lax.Precision.HIGHEST, preferred_element_type=jnp.float32)


def masked_scores(queries, keys_all, length):
    scores = jnp.einsum(
        "qhd,khd->hqk", queries, keys_all, preferred_element_type=jnp.float32
    ) * HEAD_DIM ** (-0.5)
    allowed = jnp.arange(SLOT) < length
    return jnp.where(allowed[None, None, :], scores, -1e30)


def attend_forward(seq_item):
    packed, length = seq_item
    queries = packed[:, 0]
    keys_all = packed[:, 1]
    values = packed[:, 2]
    scores = masked_scores(queries, keys_all, length)
    row_max = jnp.max(scores, axis=-1, keepdims=True)
    exp_sum = jnp.sum(jnp.exp(scores - row_max), axis=-1, keepdims=True)
    log_total = row_max + jnp.log(exp_sum)
    weights = jnp.exp(scores - log_total).astype(jnp.bfloat16)
    context = jnp.einsum("hqk,khd->qhd", weights, values, preferred_element_type=jnp.float32)
    return (context.astype(jnp.bfloat16), log_total)


def attend_backward(seq_item):
    packed, log_total, d_context, length = seq_item
    queries = packed[:, 0]
    keys_all = packed[:, 1]
    values = packed[:, 2]
    scores = masked_scores(queries, keys_all, length)
    weights = jnp.exp(scores - log_total)
    weights_low = weights.astype(jnp.bfloat16)
    d_weights = jnp.einsum("qhd,khd->hqk", d_context, values, preferred_element_type=jnp.float32)
    d_values = jnp.einsum(
        "hqk,qhd->khd", weights_low, d_context, preferred_element_type=jnp.float32
    )
    row_dot = jnp.sum(weights * d_weights, axis=-1, keepdims=True)
    d_scores = (weights * (d_weights - row_dot)).astype(jnp.bfloat16)
    d_queries = jnp.einsum(
        "hqk,khd->qhd", d_scores, keys_all, preferred_element_type=jnp.float32
    ) * HEAD_DIM ** (-0.5)
    d_keys = jnp.einsum(
        "hqk,qhd->khd", d_scores, queries, preferred_element_type=jnp.float32
    ) * HEAD_DIM ** (-0.5)
    return jnp.stack([d_queries, d_keys, d_values], axis=1).astype(jnp.bfloat16)


def per_device(
    tokens,
    cotangent,
    lengths,
    labels,
    w_qkv,
    w_out,
    w_up,
    w_down,
    w_pool,
    w_class,
    biases,
    norm_gains,
    bias_up,
):
    head_parts = lax.axis_size("head")
    head_rank = lax.axis_index("head")
    tok_rows = tokens.shape[0]
    own_seqs = tok_rows // SLOT
    local_heads = HEADS // head_parts
    slice_width = D // head_parts
    own_lengths = lax.dynamic_slice_in_dim(lengths, head_rank * own_seqs, own_seqs)
    own_labels = lax.dynamic_slice_in_dim(labels, head_rank * own_seqs, own_seqs)
    slot_live = (
        (jnp.arange(SLOT)[None, :] < own_lengths[:, None]).reshape(tok_rows).astype(jnp.float32)
    )
    zeros_key = jnp.zeros((D,), jnp.float32)
    packed = jnp.dot(tokens, w_qkv, preferred_element_type=jnp.float32) + jnp.concatenate(
        [biases[0], zeros_key, biases[1]]
    )
    packed_low = packed.astype(jnp.bfloat16)
    head_view = lax.all_to_all(
        packed_low.reshape(tok_rows, 3, head_parts, slice_width),
        "head",
        split_axis=2,
        concat_axis=0,
        tiled=True,
    )
    seq_view = head_view.reshape(head_parts * own_seqs, SLOT, 3, local_heads, HEAD_DIM)
    context, log_total = lax.map(attend_forward, (seq_view, lengths))
    context_back = lax.all_to_all(
        context.reshape(head_parts * tok_rows, 1, slice_width),
        "head",
        split_axis=0,
        concat_axis=1,
        tiled=True,
    )
    context_tok = context_back.reshape(tok_rows, D)
    attn = jnp.dot(context_tok, w_out, preferred_element_type=jnp.float32) + biases[2]
    first_sum = tokens.astype(jnp.float32) + attn
    norm_one, first_pull = jax.vjp(layer_norm, first_sum, norm_gains[0], biases[3])
    norm_low = norm_one.astype(jnp.bfloat16)
    hidden_up = jnp.dot(norm_low, w_up, preferred_element_type=jnp.float32) + bias_up
    activated_full, gelu_pull = jax.vjp(exact_gelu, hidden_up)
    activated = activated_full.astype(jnp.bfloat16)
    branch = jnp.dot(activated, w_down, preferred_element_type=jnp.float32) + biases[4]
    out_full, second_pull = jax.vjp(layer_norm, norm_one + branch, norm_gains[1], biases[5])
    leading = out_full.reshape(own_seqs, SLOT, D)[:, 0].astype(jnp.bfloat16)
    pooled = jnp.tanh(jnp.dot(leading, w_pool, preferred_element_type=jnp.float32) + biases[6])
    pooled_low = pooled.astype(jnp.bfloat16)
    logits = against(pooled_low, w_class)
    onehot = (jnp.arange(CLASSES)[None, :] == own_labels[:, None]).astype(jnp.float32)
    losses = jax.nn.logsumexp(logits, axis=-1) - jnp.sum(onehot * logits, axis=-1)
    d_logits = jax.nn.softmax(logits, axis=-1) - onehot
    g_class = exact(d_logits.T, pooled_low.astype(jnp.float32))
    d_pre = exact(d_logits, w_class.astype(jnp.float32)) * (1.0 - pooled * pooled)
    g_pool = exact(leading.astype(jnp.float32).T, d_pre)
    g_pool_bias = jnp.sum(d_pre, axis=0)
    d_leading = exact(d_pre, w_pool.astype(jnp.float32).T)
    d_out = cotangent.astype(jnp.float32) * slot_live[:, None]
    d_out = d_out.reshape(own_seqs, SLOT, D).at[:, 0].add(d_leading).reshape(tok_rows, D)
    d_h2, g_gain_two, g_shift_two = second_pull(d_out)
    d_branch = d_h2.astype(jnp.bfloat16)
    g_bias_down = jnp.sum(d_branch.astype(jnp.float32), axis=0)
    g_down = inner(activated, d_branch)
    d_activated = against(d_branch, w_down)
    d_up = gelu_pull(d_activated)[0].astype(jnp.bfloat16)
    g_bias_up = jnp.sum(d_up.astype(jnp.float32), axis=0)
    g_up = inner(norm_low, d_up)
    d_norm_one = d_h2 + against(d_up, w_up)
    d_h1, g_gain_one, g_shift_one = first_pull(d_norm_one)
    d_attn = d_h1.astype(jnp.bfloat16)
    g_bias_out = jnp.sum(d_attn.astype(jnp.float32), axis=0)
    g_out = inner(context_tok, d_attn)
    d_context = against(d_attn, w_out).astype(jnp.bfloat16)
    d_context_heads = lax.all_to_all(
        d_context.reshape(tok_rows, head_parts, slice_width),
        "head",
        split_axis=1,
        concat_axis=0,
        tiled=True,
    )
    d_context_seq = d_context_heads.reshape(head_parts * own_seqs, SLOT, local_heads, HEAD_DIM)
    d_seq = lax.map(attend_backward, (seq_view, log_total, d_context_seq, lengths))
    d_back = lax.all_to_all(
        d_seq.reshape(head_parts * tok_rows, 3, 1, slice_width),
        "head",
        split_axis=0,
        concat_axis=2,
        tiled=True,
    )
    d_packed = d_back.reshape(tok_rows, 3 * D)
    g_qkv = inner(tokens, d_packed)
    column_sums = jnp.sum(d_packed.astype(jnp.float32), axis=0)
    grad_tokens = (d_h1 + against(d_packed, w_qkv)).astype(jnp.bfloat16)
    g_biases = jnp.stack(
        [column_sums[:D], column_sums[2 * D :], g_bias_out, g_shift_one, g_bias_down, g_shift_two]
    )
    g_gains = jnp.stack([g_gain_one, g_gain_two])
    g_qkv, g_out, g_up, g_down, g_pool, g_class, g_biases, g_gains, g_bias_up, g_pool_bias = (
        lax.psum_scatter(g_qkv, ("batch", "head"), scatter_dimension=1, tiled=True),
        lax.psum_scatter(g_out, ("batch", "head"), scatter_dimension=1, tiled=True),
        lax.psum_scatter(g_up, ("batch", "head"), scatter_dimension=1, tiled=True),
        lax.psum_scatter(g_down, ("batch", "head"), scatter_dimension=1, tiled=True),
        lax.psum_scatter(g_pool, ("batch", "head"), scatter_dimension=1, tiled=True),
        lax.psum_scatter(g_class, ("batch", "head"), scatter_dimension=1, tiled=True),
        lax.psum_scatter(g_biases, ("batch", "head"), scatter_dimension=1, tiled=True),
        lax.psum_scatter(g_gains, ("batch", "head"), scatter_dimension=1, tiled=True),
        lax.psum_scatter(g_bias_up, ("batch", "head"), scatter_dimension=0, tiled=True),
        lax.psum_scatter(g_pool_bias, ("batch", "head"), scatter_dimension=0, tiled=True),
    )
    return (
        out_full.astype(jnp.bfloat16),
        grad_tokens,
        losses,
        g_qkv,
        g_out,
        g_up,
        g_down,
        g_pool,
        g_class,
        g_biases,
        g_gains,
        g_bias_up,
        g_pool_bias,
    )


def solution(mesh):
    return jax.shard_map(
        per_device,
        mesh=mesh,
        in_specs=(
            P(("batch", "head"), None),
            P(("batch", "head"), None),
            P("batch"),
            P("batch"),
            P(),
            P(),
            P(),
            P(),
            P(),
            P(),
            P(),
            P(),
            P(),
        ),
        out_specs=(
            P(("batch", "head"), None),
            P(("batch", "head"), None),
            P(("batch", "head")),
            P(None, ("batch", "head")),
            P(None, ("batch", "head")),
            P(None, ("batch", "head")),
            P(None, ("batch", "head")),
            P(None, ("batch", "head")),
            P(None, ("batch", "head")),
            P(None, ("batch", "head")),
            P(None, ("batch", "head")),
            P(("batch", "head")),
            P(("batch", "head")),
        ),
        check_vma=False,
    )
```

profile of v0, /device:TPU:0, one launch (start us, length us, event | category | flops | bytes accessed | tf_op | source)
XLA Modules:
  0.0 791.8 jit_solution(17786111128805935081)
XLA Ops:
  9.3 4.5 fusion.34
  13.8 4.3 copy.63
  18.1 3.2 copy.64
  21.3 4.7 all-to-all-start
  26.0 29.1 %all-to-all-done = bf16[512,3,4,192]{0,3,1,2:T(8,128)(2,1)} async-done(((bf16[512,3,4,192]{0,3,1,2:T(8,128)(2,1)}), bf16[512,3,4,192]{0,3,1,2:T(8,128)(2,1)}, u32[]{:S(2)}, u32[]{:S(2)}) %all-to-all-start) | async-done | bytes 2359328 | tf_op jit(solution)/shard_map/all_to_all | solution.py:115
  55.1 24.0 %while.23 = (s32[]{:T(128)}, bf16[4,512,3,64]{1,3,2,0:T(8,128)(2,1)}, f32[4,3,512,1]{2,1,3,0:T(4,128)}, bf16[4,512,3,3,64]{1,4,3,2,0:T(8,128)(2,1)}, s32[4]{0:T(128)S(1)}, /*index=5*/s32[]{:T(128)}) while((s32[]{:T(128)}, bf16[4,512,3,64]{1,3,2,0:T(8,128)(2,1)}, f32[4,3,512,1]{2,1,3,0:T(4,128)}, bf16[4,512,3,3,64]{1,4,3,2,0:T(8,128)(2,1)}, ...), condition=%wide.region_3.4_spmd, body=%wide.region_0.3_spmd.sunk | while | flops 210074624 | bytes 11459673 | solution.py:123
  90.3 3.9 reshape.384
  94.3 4.2 all-to-all-start.1
  104.6 5.5 all-to-all-done.1
  110.2 4.1 reshape.385
  114.3 5.7 copy.67
  128.2 19.6 %multiply_convert_fusion.1 = (bf16[512,3072]{1,0:T(8,128)(2,1)S(1)}, f32[512,3072]{1,0:T(8,128)}, f32[512,3072]{1,0:T(8,128)}) fusion(f32[3072]{0:T(1024)S(1)} %copy-done.37, bf16[768,3072]{1,0:T(8,128)(2,1)} %param.25, f32[512,768]{1,0:T(8,128)S(1)} %get-tuple-element.165, f32[768]{0:T(1024)S(1)} %copy-done.32, f32[768]{0:T(1024)S(1)} %get-tuple-element.176, ...), kind=kOutput, calls=%fused_computation.50 | convolution fusion | flops 2521694208 | bytes 22042624 | tf_op jit(solution)/shard_map/dot_general | solution.py:136
  163.2 3.2 multiply_reduce_fusion.1
  172.7 9.5 %convert_reduce_fusion = (f32[3072]{0:T(1024)}, bf16[512,3072]{1,0:T(8,128)(2,1)S(1)}) fusion(f32[512,3072]{1,0:T(8,128)} %get-tuple-element.156, f32[512,3072]{1,0:T(8,128)} %get-tuple-element.166, f32[3072]{0:T(1024)} %param.31, bf16[512,768]{1,0:T(8,128)(2,1)S(1)} %get-tuple-element.148, bf16[3072,768]{1,0:T(8,128)(2,1)} %param.26), kind=kOutput, calls=%fused_computation.48 | convolution fusion | flops 2442654720 | bytes 21258240 | tf_op jit(solution)/shard_map/dot_general | solution.py:30
  182.2 7.3 multiply_reduce_fusion.2
  196.5 4.2 all-to-all-start.2
  200.9 3.6 fusion.60
  204.6 7.8 all-to-all-done.2
  212.4 39.9 %while.24 = (s32[]{:T(128)}, bf16[4,512,3,3,64]{1,4,3,2,0:T(8,128)(2,1)}, bf16[4,512,3,3,64]{1,4,3,2,0:T(8,128)(2,1)}, s32[4]{0:T(128)}, f32[4,3,512,1]{2,1,3,0:...) while((s32[]{:T(128)}, bf16[4,512,3,3,64]{1,4,3,2,0:T(8,128)(2,1)}, ...), condition=%wide.region_16.17_spmd, body=%wide.region_14.16_spmd.sunk | while | flops 512654336 | bytes 27953856 | solution.py:177
  252.3 4.9 copy.70
  257.2 5.9 reshape.346
  263.1 7.0 copy.71
  270.0 53.9 %all_to_all.60 = bf16[2048,3,1,192]{3,1,2,0:T(4,128)(2,1)} all-to-all(bf16[2048,3,1,192]{3,1,2,0:T(4,128)(2,1)} %copy.71), channel_id=1, replica_groups=mesh['batch'=8,'head'=4] {'head'}, dimensions={0} | all-to-all | bytes 4718592 | tf_op jit(solution)/shard_map/all_to_all | solution.py:178
  323.9 7.4 copy.80
  335.0 5.0 convolution_bitcast_fusion
  340.2 8.8 %fusion.48 = f32[768,3072]{0,1:T(8,128)} fusion(bf16[512,3072]{1,0:T(8,128)(2,1)} %copy-done.43, f32[512,768]{1,0:T(8,128)} %copy-done.6, f32[768]{0:T(1024)} %get-tuple-element.107, f32[768]{0:T(1024)S(1)} %copy-done.27, f32[512]{0:T(512)} %copy-done.28, f32[512]{0:T(512)S(1)} %copy-done.17), kind=kOutput, calls=%fused_computation.138 | convolution fusion | flops 2417885184 | bytes 14166016 | tf_op jit(solution)/shard_map/dot_general | solution.py:24
  349.1 8.4 %fusion.61 = f32[3072,768]{0,1:T(8,128)} fusion(bf16[512,3072]{1,0:T(8,128)(2,1)} %copy-done.42, bf16[512,768]{1,0:T(8,128)(2,1)} %copy-done.13), kind=kOutput, calls=%fused_computation.148 | convolution fusion | flops 2415919104 | bytes 13369344 | tf_op jit(solution)/shard_map/dot_general | solution.py:24
  375.8 42.2 %all-reduce.5 = (f32[3,768]{1,0:T(4,128)}, f32[6,768]{1,0:T(8,128)}, f32[2,768]{1,0:T(2,128)}, f32[3072]{0:T(1024)}, f32[768]{0:T(1024)}) all-reduce(f32[3,768]{1,0:T(4,128)S(1)} %broadcast_multiply_fusion.1, f32[6,768]{1,0:T(8,128)} %stack.38, ...), channel_id=7, replica_groups=mesh['batch'=8,'head'=4] {'batch','head'}, use_global_device_ids=true, to_apply=%region_24.25.clone | all-reduce | flops 12288 | bytes 98304
  424.6 5.1 add_convert_fusion.1
  429.7 70.9 %reduce-scatter.9.cloned.1.call-done = f32[768,72]{0,1:T(8,128)} async-done(((f32[768,2304]{0,1:T(8,128)}), f32[768,72]{0,1:T(8,128)}) %reduce-scatter.9.cloned.1.call-update) | async-done | bytes 221200 | tf_op jit(solution)/shard_map/reduce_scatter | solution.py:194
  500.6 142.2 %reduce-scatter.13.cloned.1.call-done = f32[768,96]{0,1:T(8,128)} async-done(((f32[768,3072]{0,1:T(8,128)}), f32[768,96]{0,1:T(8,128)}) %reduce-scatter.13.cloned.1.call-update) | async-done | bytes 294928 | tf_op jit(solution)/shard_map/reduce_scatter | solution.py:196
  642.8 140.9 %reduce-scatter.15.cloned.1.call-done = f32[3072,24]{0,1:T(8,128)} async-done(((f32[3072,768]{0,1:T(8,128)}), f32[3072,24]{0,1:T(8,128)}) %reduce-scatter.15.cloned.1.call-update) | async-done | bytes 294928 | tf_op jit(solution)/shard_map/reduce_scatter | solution.py:197
  (254 shorter events, 146.0 us)
Async XLA Ops:
  8.8 139.0 %copy-start.26 = (f32[768]{0:T(1024)}, f32[768]{0:T(1024)S(1)}, u32[]{:S(2)}) copy-start(f32[768]{0:T(1024)S(1)} %get-tuple-element.176) | copy-start | bytes 9220
  21.3 33.8 %copy-start.40 = (s32[4]{0:T(128)S(1)}, s32[4]{0:T(128)}, u32[]{:S(2)}) copy-start(s32[4]{0:T(128)} %param.21) | copy-start | bytes 52
  21.3 33.8 %all-to-all-start = ((bf16[512,3,4,192]{0,3,1,2:T(8,128)(2,1)}), bf16[512,3,4,192]{0,3,1,2:T(8,128)(2,1)}, u32[]{:S(2)}, u32[]{:S(2)}) async-start(bf16[512,3,4,192]{0,3,1,2:T(8,128)(2,1)} %copy.64), calls=%async_computation | async-start | bytes 4718592 | tf_op jit(solution)/shard_map/all_to_all | solution.py:115
  85.1 15.2 %copy-start.39 = (s32[4]{0:T(128)S(1)}, s32[4]{0:T(128)}, u32[]{:S(2)}) copy-start(s32[4]{0:T(128)} %param.22) | copy-start | bytes 52
  94.3 15.9 %all-to-all-start.1 = ((bf16[4,2,49152]{2,1,0:T(2,128)(2,1)}), bf16[4,2,49152]{2,1,0:T(2,128)(2,1)}, u32[]{:S(2)}, u32[]{:S(2)}) async-start(bf16[4,2,49152]{2,1,0:T(2,128)(2,1)} %reshape.384), calls=%async_computation.1 | async-start | bytes 1572864 | tf_op jit(solution)/shard_map/all_to_all | solution.py:124
  98.5 331.2 %reduce-scatter.17.cloned.1.call-start = ((), (), s32[]{:S(2)}) async-start(), calls=%async_computation.13 | async-start | bytes 2433024 | tf_op jit(solution)/shard_map/reduce_scatter | solution.py:198
  114.3 10.0 %copy-start.34 = (f32[768]{0:T(1024)S(1)}, f32[768]{0:T(1024)}, u32[]{:S(2)}) copy-start(f32[768]{0:T(1024)} %get-tuple-element.108) | copy-start | bytes 9220
  124.3 3.9 copy-start.32
  124.4 23.6 %slice-start = ((s8[4718592]{0:T(1024)(128)(4,1)}), s8[4194304]{0:T(1024)(128)(4,1)S(1)}, s32[]{:S(2)}) async-start(s8[4718592]{0:T(1024)(128)(4,1)} %bitcast.202), calls=%async_computation.14 | async-start | bytes 8388608
  127.1 20.8 %copy-start.6 = (f32[512,768]{1,0:T(8,128)}, f32[512,768]{1,0:T(8,128)S(1)}, u32[]{:S(2)}) copy-start(f32[512,768]{1,0:T(8,128)S(1)} %get-tuple-element.165) | copy-start | bytes 4718596
  127.1 20.8 %copy-start.16 = (f32[512]{0:T(512)}, f32[512]{0:T(512)S(1)}, u32[]{:S(2)}) copy-start(f32[512]{0:T(512)S(1)} %broadcast_multiply_fusion.3) | copy-start | bytes 6148
  128.2 19.7 %copy-start.28 = (f32[512]{0:T(512)}, f32[512]{0:T(512)S(1)}, u32[]{:S(2)}) copy-start(f32[512]{0:T(512)S(1)} %fusion.43) | copy-start | bytes 6148
  128.2 19.7 %copy-start.33 = (f32[768]{0:T(1024)S(1)}, f32[768]{0:T(1024)}, u32[]{:S(2)}) copy-start(f32[768]{0:T(1024)} %get-tuple-element.106) | copy-start | bytes 9220
  128.2 19.7 %slice-start.1 = ((s8[4718592]{0:T(1024)(128)(4,1)}), s8[524288]{0:T(1024)(128)(4,1)S(1)}, s32[]{:S(2)}) async-start(s8[4718592]{0:T(1024)(128)(4,1)} %bitcast.202), calls=%async_computation.15 | async-start | bytes 1048576
  150.7 10.5 %copy-start.1 = (f32[512,768]{1,0:T(8,128)}, f32[512,768]{1,0:T(8,128)S(1)}, u32[]{:S(2)}) copy-start(f32[512,768]{1,0:T(8,128)S(1)} %get-tuple-element.168) | copy-start | bytes 4718596
  150.8 10.5 %copy-start.25 = (f32[768]{0:T(1024)S(1)}, f32[768]{0:T(1024)}, u32[]{:S(2)}) copy-start(f32[768]{0:T(1024)} %slice_reduce_fusion) | copy-start | bytes 9220
  163.2 3.9 copy-start.2
  163.2 3.9 copy-start.4
  172.6 9.6 %copy-start.13 = (bf16[512,768]{1,0:T(8,128)(2,1)}, bf16[512,768]{1,0:T(8,128)(2,1)S(1)}, u32[]{:S(2)}) copy-start(bf16[512,768]{1,0:T(8,128)(2,1)S(1)} %get-tuple-element.148) | copy-start | bytes 2359300
  172.6 9.6 %copy-start.7 = (f32[512,768]{1,0:T(8,128)S(1)}, f32[512,768]{1,0:T(8,128)}, u32[]{:S(2)}) copy-start(f32[512,768]{1,0:T(8,128)} %copy-done.6) | copy-start | bytes 4718596
  172.6 9.6 %copy-start.9 = (f32[512,768]{1,0:T(8,128)S(1)}, f32[512,768]{1,0:T(8,128)}, u32[]{:S(2)}) copy-start(f32[512,768]{1,0:T(8,128)} %get-tuple-element.154) | copy-start | bytes 4718596
  172.7 9.6 %copy-start.17 = (f32[512]{0:T(512)S(1)}, f32[512]{0:T(512)}, u32[]{:S(2)}) copy-start(f32[512]{0:T(512)} %copy-done.16) | copy-start | bytes 6148
  172.7 9.5 %copy-start.27 = (f32[768]{0:T(1024)S(1)}, f32[768]{0:T(1024)}, u32[]{:S(2)}) copy-start(f32[768]{0:T(1024)} %copy-done.26) | copy-start | bytes 9220
  172.7 9.5 %copy-start.29 = (f32[512]{0:T(512)S(1)}, f32[512]{0:T(512)}, u32[]{:S(2)}) copy-start(f32[512]{0:T(512)} %copy-done.28) | copy-start | bytes 6148
  182.2 7.3 copy-start.43
  182.2 7.3 copy-start.19
  196.5 15.9 %all-to-all-start.2 = ((bf16[512,4,192]{0,2,1:T(8,128)(2,1)}), bf16[512,4,192]{0,2,1:T(8,128)(2,1)}, u32[]{:S(2)}, u32[]{:S(2)}) async-start(bf16[512,4,192]{0,2,1:T(8,128)(2,1)} %bitcast.198), calls=%async_computation.2 | async-start | bytes 1572864 | tf_op jit(solution)/shard_map/all_to_all | solution.py:169
  200.7 229.0 %reduce-scatter.11.cloned.1.call-start = ((), (), s32[]{:S(2)}) async-start(), calls=%async_computation.10 | async-start | bytes 2433024 | tf_op jit(solution)/shard_map/reduce_scatter | solution.py:195
  204.6 296.0 %reduce-scatter.9.cloned.1.call-start = ((), (), s32[]{:S(2)}) async-start(), calls=%async_computation.9 | async-start | bytes 7299072 | tf_op jit(solution)/shard_map/reduce_scatter | solution.py:194
  339.9 302.9 %reduce-scatter.13.cloned.1.call-start = ((), (), s32[]{:S(2)}) async-start(), calls=%async_computation.11 | async-start | bytes 9732096 | tf_op jit(solution)/shard_map/reduce_scatter | solution.py:196
  349.1 434.6 %reduce-scatter.15.cloned.1.call-start = ((), (), s32[]{:S(2)}) async-start(), calls=%async_computation.12 | async-start | bytes 9732096 | tf_op jit(solution)/shard_map/reduce_scatter | solution.py:197
  358.2 17.6 %copy-start.24 = (f32[768]{0:T(1024)S(1)}, f32[768]{0:T(1024)}, u32[]{:S(2)}) copy-start(f32[768]{0:T(1024)} %get-tuple-element.172) | copy-start | bytes 9220
  (25 other events, 59.5 us)
Sparse Core Ops, SparseCore 0:
  171.1 100.1 reduce-scatter.16
  278.1 98.0 reduce-scatter.10
  382.4 118.0 reduce-scatter.8
  507.9 134.8 reduce-scatter.12
  649.1 134.5 reduce-scatter.14
where the time goes:
time: 800 us; the launch traced here: 792 us
  waiting for transfers between devices  397 us (50%)
  matrix products  112 us (14%)
  local copies, waits for them, and re-layouts  111 us (14%)
  blocking collectives  96.1 us (12%)
  other arithmetic  42.7 us (5%)
  between operations  18.5 us (2%)
  starting transfers between devices  14.2 us (2%)
    reduce_scatter x1, waiting for transfers between devices, per_device(): lax.psum_scatter(g_up, ('batch', 'head'), scatter_dimension=1, tiled=True)  142 us
    reduce_scatter x1, waiting for transfers between devices, per_device(): lax.psum_scatter(g_down, ('batch', 'head'), scatter_dimension=1, tiled=True)  141 us
    reduce_scatter x1, waiting for transfers between devices, per_device(): lax.psum_scatter(g_qkv, ('batch', 'head'), scatter_dimension=1, tiled=True)  70.9 us
    all_to_all x1, blocking collectives, per_device(): lax.all_to_all(d_seq.reshape(head_parts * tok_rows, 3, 1, slice_width), '...  53.9 us
    unnamed x1, blocking collectives  42.2 us
    all_to_all x1, waiting for transfers between devices, per_device(): lax.all_to_all(packed_low.reshape(tok_rows, 3, head_parts, slice_width),...  29.1 us
    dot_general x4, matrix products, inner(): lax.dot_general(left, right, (((0,), (0,)), ((), ())), preferred_element_...  25.8 us
    dot_general x5, matrix products, against(): lax.dot_general(left, right, (((1,), (1,)), ((), ())), preferred_element_...  24.3 us
  transfers between devices with their start and end apart: 8, of which 6 were waited for; matrix products, arithmetic and copies ran while one was open for 19% of the time, Pallas kernels for 0%

commit v1 on v0

--- a/solution.py
+++ b/solution.py
@@ -121,13 +121,20 @@
     )
     seq_view = head_view.reshape(head_parts * own_seqs, SLOT, 3, local_heads, HEAD_DIM)
     context, log_total = lax.map(attend_forward, (seq_view, lengths))
-    context_back = lax.all_to_all(
-        context.reshape(head_parts * tok_rows, 1, slice_width),
-        "head",
-        split_axis=0,
-        concat_axis=1,
-        tiled=True,
-    )
+    x = context.reshape(head_parts * tok_rows, 1, slice_width)
+    ways, here = (lax.axis_size("head"), lax.axis_index("head"))
+    width = x.shape[0] // ways
+    lengths_2 = list(x.shape)
+    lengths_2[0] = width
+    height = lengths_2[1]
+    lengths_2[1] = height * ways
+    full = jnp.zeros(lengths_2, x.dtype)
+    for mask in range(ways):
+        part = lax.dynamic_slice_in_dim(x, (here ^ mask) * width, width, axis=0)
+        if mask:
+            part = lax.ppermute(part, "head", [(d, d ^ mask) for d in range(ways)])
+        full = lax.dynamic_update_slice_in_dim(full, part, (here ^ mask) * height, axis=1)
+    context_back = full
     context_tok = context_back.reshape(tok_rows, D)
     attn = jnp.dot(context_tok, w_out, preferred_element_type=jnp.float32) + biases[2]
     first_sum = tokens.astype(jnp.float32) + attn

time: 800 us -> 779 us (0.974)
  local copies, waits for them, and re-layouts: 111 us -> 98 us
    unnamed x98 -> x85, local copies, waits for them, and re-layouts: 23.3 us -> 11.9 us
    all_to_all x3 -> x0, local copies, waits for them, and re-layouts: 9.99 us -> none  [per_device(): lax.all_to_all(context.reshape(head_parts * tok_rows, 1, slice_width), 'h...]
  transfers between devices with their start and end apart: 8 -> 10, of which waited for: 6 -> 7; matrix products, arithmetic and copies ran while one was open for 19% -> 20% of each run, Pallas kernels for 0% -> 0%
where the time goes in v1:
time: 779 us; the launch traced here: 774 us
  waiting for transfers between devices  396 us (51%)
  matrix products  113 us (15%)
  local copies, waits for them, and re-layouts  98 us (13%)
  blocking collectives  96.3 us (12%)
  other arithmetic  40.8 us (5%)
  between operations  18.3 us (2%)
  starting transfers between devices  11.7 us (2%)
    reduce_scatter x1, waiting for transfers between devices, per_device(): lax.psum_scatter(g_up, ('batch', 'head'), scatter_dimension=1, tiled=True)  142 us
    reduce_scatter x1, waiting for transfers between devices, per_device(): lax.psum_scatter(g_down, ('batch', 'head'), scatter_dimension=1, tiled=True)  141 us
    reduce_scatter x1, waiting for transfers between devices, per_device(): lax.psum_scatter(g_qkv, ('batch', 'head'), scatter_dimension=1, tiled=True)  70.7 us
    all_to_all x1, blocking collectives, per_device(): lax.all_to_all(d_seq.reshape(head_parts * tok_rows, 3, 1, slice_width), '...  53.9 us
    unnamed x1, blocking collectives  42.4 us
    all_to_all x1, waiting for transfers between devices, per_device(): lax.all_to_all(packed_low.reshape(tok_rows, 3, head_parts, slice_width),...  27.5 us
    dot_general x4, matrix products, inner(): lax.dot_general(left, right, (((0,), (0,)), ((), ())), preferred_element_...  25.8 us
    dot_general x5, matrix products, against(): lax.dot_general(left, right, (((1,), (1,)), ((), ())), preferred_element_...  24.3 us
  transfers between devices with their start and end apart: 10, of which 7 were waited for; matrix products, arithmetic and copies ran while one was open for 20% of the time, Pallas kernels for 0%

profile of v1, /device:TPU:0, one launch (start us, length us, event | category | flops | bytes accessed | tf_op | source)
XLA Modules:
  0.0 773.8 jit_solution(1841734559492779505)
XLA Ops:
  9.3 4.5 fusion.34
  13.9 4.3 copy.59
  18.1 3.2 copy.60
  21.4 4.7 all-to-all-start
  27.7 27.5 %all-to-all-done = bf16[512,3,4,192]{0,3,1,2:T(8,128)(2,1)} async-done(((bf16[512,3,4,192]{0,3,1,2:T(8,128)(2,1)}), bf16[512,3,4,192]{0,3,1,2:T(8,128)(2,1)}, u32[]{:S(2)}, u32[]{:S(2)}) %all-to-all-start) | async-done | bytes 2359328 | tf_op jit(solution)/shard_map/all_to_all | solution.py:115
  55.2 26.6 %while.23 = (s32[]{:T(128)}, bf16[4,512,3,64]{1,3,2,0:T(8,128)(2,1)}, f32[4,3,512,1]{2,1,3,0:T(4,128)}, bf16[4,512,3,3,64]{1,4,3,2,0:T(8,128)(2,1)}, s32[4]{0:T(128)}, /*index=5*/s32[]{:T(128)}) while((s32[]{:T(128)}, bf16[4,512,3,64]{1,3,2,0:T(8,128)(2,1)}, f32[4,3,512,1]{2,1,3,0:T(4,128)}, bf16[4,512,3,3,64]{1,4,3,2,0:T(8,128)(2,1)}, ...), condition=%wide.region_3.4_spmd, body=%wide.region_0.3_spmd.sunk | while | flops 210074624 | bytes 11459673 | solution.py:123
  84.4 2.8 reshape.336
  98.3 3.6 collective-permute-done.1
  102.6 2.7 collective-permute-done.2
  106.0 2.8 fusion.56
  110.0 20.0 %multiply_convert_fusion.1 = (bf16[512,3072]{1,0:T(8,128)(2,1)S(1)}, f32[512,3072]{1,0:T(8,128)}, f32[512,3072]{1,0:T(8,128)}) fusion(f32[3072]{0:T(1024)S(1)} %copy-done.33, bf16[768,3072]{1,0:T(8,128)(2,1)} %param.25, f32[512,768]{1,0:T(8,128)S(1)} %get-tuple-element.169, f32[768]{0:T(1024)S(1)} %copy-done.29, f32[768]{0:T(1024)S(1)} %get-tuple-element.180, ...), kind=kOutput, calls=%fused_computation.50 | convolution fusion | flops 2521694208 | bytes 22042624 | tf_op jit(solution)/shard_map/dot_general | solution.py:143
  130.1 2.8 fusion.57
  145.4 3.2 multiply_reduce_fusion.1
  154.8 9.5 %convert_reduce_fusion = (f32[3072]{0:T(1024)}, bf16[512,3072]{1,0:T(8,128)(2,1)S(1)}) fusion(f32[512,3072]{1,0:T(8,128)} %get-tuple-element.156, f32[512,3072]{1,0:T(8,128)} %get-tuple-element.170, f32[3072]{0:T(1024)} %param.31, bf16[512,768]{1,0:T(8,128)(2,1)S(1)} %get-tuple-element.148, bf16[3072,768]{1,0:T(8,128)(2,1)} %param.26), kind=kOutput, calls=%fused_computation.48 | convolution fusion | flops 2442654720 | bytes 21258240 | tf_op jit(solution)/shard_map/dot_general | solution.py:30
  164.4 7.2 multiply_reduce_fusion.2
  178.6 4.2 all-to-all-start.1
  183.0 3.6 fusion.60
  186.7 7.8 %all-to-all-done.1 = bf16[512,4,192]{0,2,1:T(8,128)(2,1)} async-done(((bf16[512,4,192]{0,2,1:T(8,128)(2,1)}), bf16[512,4,192]{0,2,1:T(8,128)(2,1)}, u32[]{:S(2)}, u32[]{:S(2)}) %all-to-all-start.1) | async-done | bytes 786464 | tf_op jit(solution)/shard_map/all_to_all | solution.py:176
  194.5 39.9 %while.24 = (s32[]{:T(128)}, bf16[4,512,3,3,64]{1,4,3,2,0:T(8,128)(2,1)}, bf16[4,512,3,3,64]{1,4,3,2,0:T(8,128)(2,1)}, s32[4]{0:T(128)}, f32[4,3,512,1]{2,1,3,0:...) while((s32[]{:T(128)}, bf16[4,512,3,3,64]{1,4,3,2,0:T(8,128)(2,1)}, ...), condition=%wide.region_16.17_spmd, body=%wide.region_14.16_spmd.sunk | while | flops 512654336 | bytes 27953856 | solution.py:184
  234.5 4.9 copy.63
  239.4 5.9 reshape.345
  245.2 7.0 copy.64
  252.2 53.9 %all_to_all.45 = bf16[2048,3,1,192]{3,1,2,0:T(4,128)(2,1)} all-to-all(bf16[2048,3,1,192]{3,1,2,0:T(4,128)(2,1)} %copy.64), channel_id=1, replica_groups=mesh['batch'=8,'head'=4] {'head'}, dimensions={0} | all-to-all | bytes 4718592 | tf_op jit(solution)/shard_map/all_to_all | solution.py:185
  306.1 7.4 copy.73
  317.1 5.0 convolution_bitcast_fusion
  322.3 8.8 %fusion.48 = f32[768,3072]{0,1:T(8,128)} fusion(bf16[512,3072]{1,0:T(8,128)(2,1)} %copy-done.38, f32[512,768]{1,0:T(8,128)} %copy-done.5, f32[768]{0:T(1024)} %get-tuple-element.107, f32[768]{0:T(1024)S(1)} %copy-done.24, f32[512]{0:T(512)} %copy-done.25, f32[512]{0:T(512)S(1)} %copy-done.15), kind=kOutput, calls=%fused_computation.145 | convolution fusion | flops 2417885184 | bytes 14166016 | tf_op jit(solution)/shard_map/dot_general | solution.py:24
  331.2 8.4 %fusion.61 = f32[3072,768]{0,1:T(8,128)} fusion(bf16[512,3072]{1,0:T(8,128)(2,1)} %copy-done.37, bf16[512,768]{1,0:T(8,128)(2,1)} %copy-done.11), kind=kOutput, calls=%fused_computation.155 | convolution fusion | flops 2415919104 | bytes 13369344 | tf_op jit(solution)/shard_map/dot_general | solution.py:24
  357.9 42.4 %all-reduce.5 = (f32[3,768]{1,0:T(4,128)}, f32[6,768]{1,0:T(8,128)}, f32[2,768]{1,0:T(2,128)}, f32[3072]{0:T(1024)}, f32[768]{0:T(1024)}) all-reduce(f32[3,768]{1,0:T(4,128)S(1)} %broadcast_multiply_fusion.1, f32[6,768]{1,0:T(8,128)} %stack.38, ...), channel_id=7, replica_groups=mesh['batch'=8,'head'=4] {'batch','head'}, use_global_device_ids=true, to_apply=%region_24.25.clone | all-reduce | flops 12288 | bytes 98304
  406.8 5.1 add_convert_fusion.1
  411.9 70.7 %reduce-scatter.9.cloned.1.call-done = f32[768,72]{0,1:T(8,128)} async-done(((f32[768,2304]{0,1:T(8,128)}), f32[768,72]{0,1:T(8,128)}) %reduce-scatter.9.cloned.1.call-update) | async-done | bytes 221200 | tf_op jit(solution)/shard_map/reduce_scatter | solution.py:201
  482.7 142.3 %reduce-scatter.13.cloned.1.call-done = f32[768,96]{0,1:T(8,128)} async-done(((f32[768,3072]{0,1:T(8,128)}), f32[768,96]{0,1:T(8,128)}) %reduce-scatter.13.cloned.1.call-update) | async-done | bytes 294928 | tf_op jit(solution)/shard_map/reduce_scatter | solution.py:203
  625.0 140.9 %reduce-scatter.15.cloned.1.call-done = f32[3072,24]{0,1:T(8,128)} async-done(((f32[3072,768]{0,1:T(8,128)}), f32[3072,24]{0,1:T(8,128)}) %reduce-scatter.15.cloned.1.call-update) | async-done | bytes 294928 | tf_op jit(solution)/shard_map/reduce_scatter | solution.py:204
  (245 shorter events, 138.1 us)
Async XLA Ops:
  8.8 121.2 %copy-start.23 = (f32[768]{0:T(1024)}, f32[768]{0:T(1024)S(1)}, u32[]{:S(2)}) copy-start(f32[768]{0:T(1024)S(1)} %get-tuple-element.180) | copy-start | bytes 9220
  21.4 5.1 copy-start.35
  21.4 33.8 %all-to-all-start = ((bf16[512,3,4,192]{0,3,1,2:T(8,128)(2,1)}), bf16[512,3,4,192]{0,3,1,2:T(8,128)(2,1)}, u32[]{:S(2)}, u32[]{:S(2)}) async-start(bf16[512,3,4,192]{0,3,1,2:T(8,128)(2,1)} %copy.60), calls=%async_computation | async-start | bytes 4718592 | tf_op jit(solution)/shard_map/all_to_all | solution.py:115
  26.0 385.9 %reduce-scatter.17.cloned.1.call-start = ((), (), s32[]{:S(2)}) async-start(), calls=%async_computation.12 | async-start | bytes 2433024 | tf_op jit(solution)/shard_map/reduce_scatter | solution.py:205
  90.2 6.4 collective-permute-start
  94.0 7.9 %collective-permute-start.1 = (bf16[512,1,192]{0,2,1:T(8,128)(2,1)}, bf16[512,1,192]{0,2,1:T(8,128)(2,1)S(1)}, u32[]{:S(2)}, u32[]{:S(2)}) collective-permute-start(bf16[512,1,192]{0,2,1:T(8,128)(2,1)} %get-tuple-element.163), channel_id=1, source_target_pairs={{0,2},{1,3},{2,0},{3,1},{4,6},{5,7},{6,4},{7,5},{8,10},{9,11},{10,... | collective-permute-start | bytes 589832 | tf_op jit(solution)/shard_map/ppermute | solution.py:135
  94.8 10.6 %collective-permute-start.2 = (bf16[512,1,192]{0,2,1:T(8,128)(2,1)}, bf16[512,1,192]{0,2,1:T(8,128)(2,1)S(1)}, u32[]{:S(2)}, u32[]{:S(2)}) collective-permute-start(bf16[512,1,192]{0,2,1:T(8,128)(2,1)} %get-tuple-element.162), channel_id=1, source_target_pairs={{0,3},{1,2},{2,1},{3,0},{4,7},{5,6},{6,5},{7,4},{8,11},{9,10},{10,... | collective-permute-start | bytes 589832 | tf_op jit(solution)/shard_map/ppermute | solution.py:135
  106.0 3.9 copy-start.29
  106.0 3.9 copy-start.33
  106.0 24.0 %slice-start = ((s8[4718592]{0:T(1024)(128)(4,1)}), s8[4194304]{0:T(1024)(128)(4,1)S(1)}, s32[]{:S(2)}) async-start(s8[4718592]{0:T(1024)(128)(4,1)} %bitcast.196), calls=%async_computation.13 | async-start | bytes 8388608
  108.9 21.2 %copy-start.5 = (f32[512,768]{1,0:T(8,128)}, f32[512,768]{1,0:T(8,128)S(1)}, u32[]{:S(2)}) copy-start(f32[512,768]{1,0:T(8,128)S(1)} %get-tuple-element.169) | copy-start | bytes 4718596
  108.9 21.2 %copy-start.14 = (f32[512]{0:T(512)}, f32[512]{0:T(512)S(1)}, u32[]{:S(2)}) copy-start(f32[512]{0:T(512)S(1)} %broadcast_multiply_fusion.3) | copy-start | bytes 6148
  110.0 20.1 %copy-start.25 = (f32[512]{0:T(512)}, f32[512]{0:T(512)S(1)}, u32[]{:S(2)}) copy-start(f32[512]{0:T(512)S(1)} %fusion.43) | copy-start | bytes 6148
  110.0 20.1 %copy-start.30 = (f32[768]{0:T(1024)S(1)}, f32[768]{0:T(1024)}, u32[]{:S(2)}) copy-start(f32[768]{0:T(1024)} %get-tuple-element.106) | copy-start | bytes 9220
  110.0 20.1 %slice-start.1 = ((s8[4718592]{0:T(1024)(128)(4,1)}), s8[524288]{0:T(1024)(128)(4,1)S(1)}, s32[]{:S(2)}) async-start(s8[4718592]{0:T(1024)(128)(4,1)} %bitcast.196), calls=%async_computation.14 | async-start | bytes 1048576
  132.9 10.5 %copy-start.1 = (f32[512,768]{1,0:T(8,128)}, f32[512,768]{1,0:T(8,128)S(1)}, u32[]{:S(2)}) copy-start(f32[512,768]{1,0:T(8,128)S(1)} %get-tuple-element.172) | copy-start | bytes 4718596
  145.4 3.9 copy-start.2
  145.4 3.9 copy-start.3
  154.8 9.6 %copy-start.11 = (bf16[512,768]{1,0:T(8,128)(2,1)}, bf16[512,768]{1,0:T(8,128)(2,1)S(1)}, u32[]{:S(2)}) copy-start(bf16[512,768]{1,0:T(8,128)(2,1)S(1)} %get-tuple-element.148) | copy-start | bytes 2359300
  154.8 9.6 %copy-start.6 = (f32[512,768]{1,0:T(8,128)S(1)}, f32[512,768]{1,0:T(8,128)}, u32[]{:S(2)}) copy-start(f32[512,768]{1,0:T(8,128)} %copy-done.5) | copy-start | bytes 4718596
  154.8 9.6 %copy-start.8 = (f32[512,768]{1,0:T(8,128)S(1)}, f32[512,768]{1,0:T(8,128)}, u32[]{:S(2)}) copy-start(f32[512,768]{1,0:T(8,128)} %get-tuple-element.154) | copy-start | bytes 4718596
  154.8 9.6 %copy-start.15 = (f32[512]{0:T(512)S(1)}, f32[512]{0:T(512)}, u32[]{:S(2)}) copy-start(f32[512]{0:T(512)} %copy-done.14) | copy-start | bytes 6148
  154.8 9.6 %copy-start.24 = (f32[768]{0:T(1024)S(1)}, f32[768]{0:T(1024)}, u32[]{:S(2)}) copy-start(f32[768]{0:T(1024)} %copy-done.23) | copy-start | bytes 9220
  154.8 9.6 %copy-start.26 = (f32[512]{0:T(512)S(1)}, f32[512]{0:T(512)}, u32[]{:S(2)}) copy-start(f32[512]{0:T(512)} %copy-done.25) | copy-start | bytes 6148
  164.3 7.3 copy-start.38
  164.4 7.3 copy-start.17
  178.6 15.9 %all-to-all-start.1 = ((bf16[512,4,192]{0,2,1:T(8,128)(2,1)}), bf16[512,4,192]{0,2,1:T(8,128)(2,1)}, u32[]{:S(2)}, u32[]{:S(2)}) async-start(bf16[512,4,192]{0,2,1:T(8,128)(2,1)} %bitcast.195), calls=%async_computation.1 | async-start | bytes 1572864 | tf_op jit(solution)/shard_map/all_to_all | solution.py:176
  182.8 229.1 %reduce-scatter.11.cloned.1.call-start = ((), (), s32[]{:S(2)}) async-start(), calls=%async_computation.9 | async-start | bytes 2433024 | tf_op jit(solution)/shard_map/reduce_scatter | solution.py:202
  186.7 296.0 %reduce-scatter.9.cloned.1.call-start = ((), (), s32[]{:S(2)}) async-start(), calls=%async_computation.8 | async-start | bytes 7299072 | tf_op jit(solution)/shard_map/reduce_scatter | solution.py:201
  322.1 302.9 %reduce-scatter.13.cloned.1.call-start = ((), (), s32[]{:S(2)}) async-start(), calls=%async_computation.10 | async-start | bytes 9732096 | tf_op jit(solution)/shard_map/reduce_scatter | solution.py:203
  331.2 434.7 %reduce-scatter.15.cloned.1.call-start = ((), (), s32[]{:S(2)}) async-start(), calls=%async_computation.11 | async-start | bytes 9732096 | tf_op jit(solution)/shard_map/reduce_scatter | solution.py:204
  340.3 17.7 %copy-start.22 = (f32[768]{0:T(1024)S(1)}, f32[768]{0:T(1024)}, u32[]{:S(2)}) copy-start(f32[768]{0:T(1024)} %get-tuple-element.176) | copy-start | bytes 9220
  (22 other events, 51.5 us)
Sparse Core Ops, SparseCore 0:
  153.3 100.2 reduce-scatter.16
  260.2 98.0 reduce-scatter.10
  364.6 118.0 reduce-scatter.8
  490.0 134.9 reduce-scatter.12
  631.3 134.5 reduce-scatter.14
